TPU v7x, 32 devices: a whole 2x2x4 slice. The times are simulated.
32 devices in a mesh: dom: 8 (over z, core), cls: 4 (over y, x).
Axes of the slice: x: 2, y: 2, z: 4, core: 2. Of those that a mesh axis runs over, the one named last changes fastest.
Arguments:
- particles: bfloat16 [768, 2048], P('dom', 'cls'), may hold values from -12 to 12
- references: float32 [32, 36, 2048], P('cls', None, 'dom'), may hold values from -0.4 to 0.4
- noise_weight: float32 [1024], replicated, may hold values from 0.5 to 2
Outputs:
- class_sums: float32 [32, 36, 2048], P('cls', None, 'dom')
- class_weight: float32 [32, 36], P('cls')
All inputs are finite; a program needn't handle non-finite values.
Results may differ from a plain program's by a relative error of at most 0.0033.
Values may be sent and summed in bfloat16 or wider, within the bound.
No kernel may reach another device: no remote copies, remote signals or barrier semaphores. Data moves between devices by JAX's collectives and lax.ppermute only.
A program may use at most 64 MiB of HBM per device.

v0:
```python
import math
import jax
import jax.numpy as jnp
from jax import lax
from jax.sharding import PartitionSpec as P

WIN = 32
BOX = 64
SHIFT_SIDE = 9


def phase_tables():
    freq = jnp.arange(WIN * WIN)
    freq_y = (freq // WIN - WIN // 2).astype(jnp.float32)
    freq_x = (freq % WIN - WIN // 2).astype(jnp.float32)
    offset = jnp.arange(SHIFT_SIDE * SHIFT_SIDE)
    shift_y = (offset // SHIFT_SIDE - SHIFT_SIDE // 2).astype(jnp.float32)
    shift_x = (offset % SHIFT_SIDE - SHIFT_SIDE // 2).astype(jnp.float32)
    theta = (
        2.0
        * math.pi
        / BOX
        * (shift_x[:, None] * freq_x[None, :] + shift_y[:, None] * freq_y[None, :])
    )
    return (jnp.cos(theta), jnp.sin(theta))


def shifted_block(real_part, imag_part, cosine, sine):
    moved_real = real_part[None] * cosine[:, None] + imag_part[None] * sine[:, None]
    moved_imag = imag_part[None] * cosine[:, None] - real_part[None] * sine[:, None]
    return jnp.concatenate([moved_real, moved_imag], axis=2).astype(jnp.bfloat16)


def on_device(particles, references, noise_weight):
    columns = lax.all_gather(particles, "cls", axis=1, tiled=True)
    quarter = WIN * WIN
    real_part = columns[:, :quarter].astype(jnp.float32)
    imag_part = columns[:, quarter:].astype(jnp.float32)
    weight_full = jnp.concatenate([noise_weight, noise_weight])
    gathered = lax.all_gather(references, "dom", axis=2, tiled=True)
    weighted = (gathered * weight_full).astype(jnp.bfloat16)
    half_norm = 0.5 * jnp.sum(gathered * gathered * weight_full, axis=2)
    classes_here = weighted.shape[0]
    rotations = weighted.shape[1]
    hypotheses = classes_here * rotations
    ref_matrix = weighted.reshape(hypotheses, -1)
    half_flat = half_norm.reshape(hypotheses)
    cosine, sine = phase_tables()
    block_shifts = 3
    blocks = cosine.shape[0] // block_shifts
    rows_here = particles.shape[0]

    def block_scores(index, ref_rows, half_rows):
        cos_block = lax.dynamic_slice_in_dim(cosine, index * block_shifts, block_shifts)
        sin_block = lax.dynamic_slice_in_dim(sine, index * block_shifts, block_shifts)
        moved = shifted_block(real_part, imag_part, cos_block, sin_block)
        flat = moved.reshape(block_shifts * rows_here, -1)
        scores = (
            lax.dot_general(
                flat, ref_rows, (((1,), (1,)), ((), ())), preferred_element_type=jnp.float32
            )
            - half_rows
        )
        return (flat, scores.reshape(block_shifts, rows_here, ref_rows.shape[0]))

    def first_pass(index, carry):
        top, total = carry
        _, scores = block_scores(index, ref_matrix, half_flat)
        new_top = jnp.maximum(top, jnp.max(scores, axis=(0, 2)))
        total = total * jnp.exp(top - new_top) + jnp.sum(
            jnp.exp(scores - new_top[None, :, None]), axis=(0, 2)
        )
        return (new_top, total)

    start = (jnp.full((rows_here,), -jnp.inf, jnp.float32), jnp.zeros((rows_here,), jnp.float32))
    top, total = lax.fori_loop(0, blocks, first_pass, start)
    global_top = lax.pmax(top, "cls")
    total = lax.psum(total * jnp.exp(top - global_top), "cls")
    top = global_top
    count = ref_matrix.shape[0]

    def second_pass(index, carry):
        sums, weights_total = carry
        flat, scores = block_scores(index, ref_matrix, half_flat)
        probs = jnp.exp(scores - top[None, :, None]) / total[None, :, None]
        probs_low = probs.astype(jnp.bfloat16).reshape(block_shifts * rows_here, count)
        sums = sums + lax.dot_general(
            probs_low, flat, (((0,), (0,)), ((), ())), preferred_element_type=jnp.float32
        )
        weights_total = weights_total + jnp.sum(probs, axis=(0, 1))
        return (sums, weights_total)

    start_two = (
        jnp.zeros((count, ref_matrix.shape[1]), jnp.float32),
        jnp.zeros((count,), jnp.float32),
    )
    sums, weights_total = lax.fori_loop(0, blocks, second_pass, start_two)
    class_sums = lax.psum_scatter(
        sums.reshape(classes_here, rotations, -1), "dom", scatter_dimension=2, tiled=True
    )
    class_weight = lax.psum(weights_total, "dom").reshape(classes_here, rotations)
    return (class_sums, class_weight)


def solution(mesh):
    placed = (P("dom", "cls"), P("cls", None, "dom"), P())
    return jax.shard_map(
        on_device,
        mesh=mesh,
        in_specs=placed,
        out_specs=(P("cls", None, "dom"), P("cls", None)),
        check_vma=False,
    )
```

profile of v0, /device:TPU:0, one launch (start us, length us, event | category | flops | bytes accessed | tf_op | source)
XLA Modules:
  0.0 489.8 jit_solution(18415613660315926192)
XLA Ops:
  8.0 11.3 %all_gather.6 = bf16[96,2048]{1,0:T(8,128)(2,1)S(1)} all-gather(bf16[96,512]{1,0:T(8,128)(2,1)} %param.7), channel_id=1, replica_groups=mesh['dom'=8,'cls'=4] {'cls'}, dimensions={1}, use_global_device_ids=true | all-gather | bytes 491520 | tf_op jit(solution)/shard_map/all_gather | solution.py:35
  20.7 2.2 fusion.19
  23.9 20.1 %all-gather.2.cloned.1.call-done = f32[8,36,2048]{2,0,1:T(8,128)} async-done(((f32[8,36,256]{2,0,1:T(8,128)}), f32[8,36,2048]{2,0,1:T(8,128)}) %all-gather.2.cloned.1.call-update) | async-done | bytes 2359312 | tf_op jit(solution)/shard_map/all_gather | solution.py:40
  50.5 2.2 reshape.155
  52.8 100.0 %while.34 = (s32[]{:T(128)}, f32[96]{0:T(128)S(1)}, f32[96]{0:T(128)S(1)}, f32[96,1024]{1,0:T(8,128)}, f32[81,1024]{1,0:T(8,128)}, /*index=5*/f32[96,1024]{1,0:T...) while((s32[]{:T(128)}, f32[96]{0:T(128)S(1)}, ...), condition=%wide.wide.region_6.7_spmd.clone, body=%wide.wide.region_1.6_spmd.clone.sunk | while | flops 344789472 | bytes 9801470 | solution.py:76
  152.8 9.8 %pmax.7 = f32[96]{0:T(128)S(1)} all-reduce(f32[96]{0:T(128)S(1)} %get-tuple-element.342), channel_id=1, replica_groups=mesh['dom'=8,'cls'=4] {'cls'}, use_global_device_ids=true, to_apply=%region_7.8 | all-reduce | flops 96 | bytes 768 | tf_op jit(solution)/shard_map/pmax | solution.py:77
  162.6 8.0 %psum.14 = f32[96]{0:T(128)S(1)} all-reduce(f32[96]{0:T(128)S(1)} %exponential_multiply_fusion), channel_id=1, replica_groups=mesh['dom'=8,'cls'=4] {'cls'}, use_global_device_ids=true, to_apply=%region_8.9 | all-reduce | flops 96 | bytes 768 | tf_op jit(solution)/shard_map/psum | solution.py:78
  170.6 272.8 %while.35 = (s32[]{:T(128)}, f32[288,2048]{1,0:T(8,128)S(1)}, f32[288]{0:T(512)S(1)}, f32[96,1024]{1,0:T(8,128)}, f32[81,1024]{1,0:T(8,128)}, /*index=5*/f32[96,...) while((s32[]{:T(128)}, f32[288,2048]{1,0:T(8,128)S(1)}, ...), condition=%wide.wide.region_11.12_spmd.clone, body=%wide.wide.region_9.11_spmd.clone.sunk | while | flops 688315712 | bytes 16369070 | solution.py:97
  204.1 2.2 fusion.59
  214.2 2.2 fusion.59
  224.3 2.2 fusion.59
  234.4 2.2 fusion.59
  244.5 2.2 fusion.59
  254.6 2.2 fusion.59
  264.7 2.2 fusion.59
  274.8 2.2 fusion.59
  285.0 2.2 fusion.59
  295.1 2.2 fusion.59
  305.2 2.2 fusion.59
  315.3 2.2 fusion.59
  325.4 2.2 fusion.59
  335.5 2.2 fusion.59
  345.6 2.2 fusion.59
  355.7 2.2 fusion.59
  365.8 2.2 fusion.59
  375.9 2.2 fusion.59
  406.2 2.2 fusion.59
  416.3 2.2 fusion.59
  426.4 2.2 fusion.59
  436.5 2.2 fusion.59
  445.2 14.5 %psum.15 = f32[8,36]{1,0:T(8,128)} all-reduce(f32[8,36]{1,0:T(8,128)S(1)} %reshape.157), channel_id=1, replica_groups=mesh['dom'=8,'cls'=4] {'dom'}, use_global_device_ids=true, to_apply=%region_13.14 | all-reduce | flops 288 | bytes 2304 | tf_op jit(solution)/shard_map/psum | solution.py:101
  459.7 21.4 %reduce-scatter.2.cloned.1.call-done = f32[8,36,256]{2,1,0:T(8,128)} async-done(((f32[8,36,2048]{2,1,0:T(8,128)}), f32[8,36,256]{2,1,0:T(8,128)}) %reduce-scatter.2.cloned.1.call-update) | async-done | bytes 294928 | tf_op jit(solution)/shard_map/reduce_scatter | solution.py:98
  (843 shorter events, 334.7 us)
Async XLA Ops:
  7.2 36.8 %all-gather.2.cloned.1.call-start = ((), (), s32[]{:S(2)}) async-start(), calls=%async_computation.1 | async-start | bytes 2654208 | tf_op jit(solution)/shard_map/all_gather | solution.py:40
  7.9 473.2 %reduce-scatter.2.cloned.1.call-start = ((), (), s32[]{:S(2)}) async-start(), calls=%async_computation.2 | async-start | bytes 2949120 | tf_op jit(solution)/shard_map/reduce_scatter | solution.py:98
  47.5 3.1 copy-start.3
  56.5 2.4 copy-start
  78.7 2.4 copy-start
  171.4 2.4 copy-start.5
  181.5 2.4 copy-start.5
  191.6 2.4 copy-start.5
  201.7 2.4 copy-start.5
  211.8 2.4 copy-start.5
  221.9 2.4 copy-start.5
  232.0 2.4 copy-start.5
  242.1 2.4 copy-start.5
  252.2 2.4 copy-start.5
  262.3 2.4 copy-start.5
  272.4 2.4 copy-start.5
  282.5 2.4 copy-start.5
  292.6 2.4 copy-start.5
  302.7 2.4 copy-start.5
  312.8 2.4 copy-start.5
  322.9 2.4 copy-start.5
  333.0 2.4 copy-start.5
  343.2 2.4 copy-start.5
  353.3 2.4 copy-start.5
  363.4 2.4 copy-start.5
  373.5 2.4 copy-start.5
  383.6 2.4 copy-start.5
  393.7 2.4 copy-start.5
  403.8 2.4 copy-start.5
  413.9 2.4 copy-start.5
  424.0 2.4 copy-start.5
  434.1 2.4 copy-start.5
  (81 other events, 195.1 us)
Sparse Core Ops, SparseCore 0:
  9.6 34.3 all-gather.1
  445.2 35.8 reduce-scatter.1
where the time goes:
time: 495 us; the launch traced here: 490 us
  local copies, waits for them, and re-layouts  144 us (29%)
  matrix products  135 us (27%)
  other arithmetic  107 us (22%)
  blocking collectives  43.6 us (9%)
  waiting for transfers between devices  42.2 us (9%)
  between operations  14.1 us (3%)
    dot_general x54, matrix products, block_scores(): lax.dot_general(flat, ref_rows, (((1,), (1,)), ((), ())), preferred_eleme...  80.1 us
    another operation x54, other arithmetic  76.2 us
    dot_general x27, matrix products, second_pass(): lax.dot_general(probs_low, flat, (((0,), (0,)), ((), ())), preferred_elem...  55.1 us
    reshape x27, local copies, waits for them, and re-layouts, block_scores(): return (flat, scores.reshape(block_shifts, rows_here, ref_rows.shape[0]))  53.6 us
    dynamic_slice x54, local copies, waits for them, and re-layouts, block_scores(): lax.dynamic_slice_in_dim(sine, index * block_shifts, block_shifts)  52.9 us
    reduce_scatter x1, waiting for transfers between devices, on_device(): lax.psum_scatter(sums.reshape(classes_here, rotations, -1), 'dom', scatte...  21.4 us
    all_gather x1, waiting for transfers between devices, on_device(): gathered = lax.all_gather(references, 'dom', axis=2, tiled=True)  20.1 us
    add x27, other arithmetic, second_pass(): weights_total = weights_total + jnp.sum(probs, axis=(0, 1))  18.6 us
  transfers between devices with their start and end apart: 2, of which 2 were waited for; matrix products, arithmetic and copies ran while one was open for 1% of the time, Pallas kernels for 0%

commit v1 on v0

--- a/solution.py
+++ b/solution.py
@@ -3,10 +3,17 @@
 import jax.numpy as jnp
 from jax import lax
 from jax.sharding import PartitionSpec as P
+from jax.lax import axis_index, axis_size, ppermute
 
 WIN = 32
 BOX = 64
 SHIFT_SIDE = 9
+
+
+def _recast_trees(my_tile, dim_i):
+    my_tile = jnp.moveaxis(my_tile, 0, dim_i)
+    a_next = my_tile.shape
+    return my_tile.reshape(*a_next[:dim_i], a_next[dim_i] * a_next[dim_i + 1], *a_next[dim_i + 2 :])
 
 
 def phase_tables():
@@ -37,7 +44,30 @@
     real_part = columns[:, :quarter].astype(jnp.float32)
     imag_part = columns[:, quarter:].astype(jnp.float32)
     weight_full = jnp.concatenate([noise_weight, noise_weight])
-    gathered = lax.all_gather(references, "dom", axis=2, tiled=True)
+    axis_n = axis_size("dom")
+    entries = []
+    tick = 0
+    while tick < axis_n:
+        entries.append((tick, (tick + 1) % axis_n))
+        tick = tick + 1
+    panels = []
+    for kk, c in entries:
+        panels.append((c, kk))
+    carry_in, back = ([], [])
+    k = 0
+    while k < axis_n - 1:
+        if k % 2 == 0:
+            v_next = ppermute(carry_in[-1] if carry_in else references, "dom", entries)
+            carry_in.append(v_next)
+        else:
+            back.append(ppermute(back[-1] if back else references, axis_name="dom", perm=panels))
+        k += 1
+    val = jnp.stack([*carry_in[::-1], references, *back])
+    block_now = axis_index("dom")
+    f_next = len(carry_in)
+    e_now = block_now - f_next
+    val = val[(jnp.arange(axis_n) - e_now) % axis_n]
+    gathered = _recast_trees(val, 2)
     weighted = (gathered * weight_full).astype(jnp.bfloat16)
     half_norm = 0.5 * jnp.sum(gathered * gathered * weight_full, axis=2)
     classes_here = weighted.shape[0]

time: 495 us -> 571 us (1.15)
  matrix products: 135 us -> 204 us
  waiting for transfers between devices: 42.2 us -> 30.1 us
  starting transfers between devices: 0.08 us -> 10.6 us
    dot_general x54, matrix products: 80.1 us -> 149 us  [block_scores(): lax.dot_general(flat, ref_rows, (((1,), (1,)), ((), ())), preferred_eleme...]
    all_gather x1 -> x0, waiting for transfers between devices: 20.1 us -> none  [on_device(): gathered = lax.all_gather(references, 'dom', axis=2, tiled=True)]
    ppermute x0 -> x7, starting transfers between devices: none -> 10.5 us  [the longest x3 10 us: on_device(): ppermute(back[-1] if back else references, axis_name='dom', perm=panels)]
    ppermute x0 -> x7, waiting for transfers between devices: none -> 10 us  [the longest x4 10 us: on_device(): v_next = ppermute(carry_in[-1] if carry_in else references, 'dom', entries)]
  transfers between devices with their start and end apart: 2 -> 8, of which waited for: 2 -> 4; matrix products, arithmetic and copies ran while one was open for 1% -> 2% of each run, Pallas kernels for 0% -> 0%
where the time goes in v1:
time: 571 us; the launch traced here: 563 us
  matrix products  204 us (36%)
  local copies, waits for them, and re-layouts  148 us (26%)
  other arithmetic  110 us (19%)
  blocking collectives  42.6 us (7%)
  waiting for transfers between devices  30.1 us (5%)
  between operations  14.1 us (2%)
  starting transfers between devices  10.6 us (2%)
    dot_general x54, matrix products, block_scores(): lax.dot_general(flat, ref_rows, (((1,), (1,)), ((), ())), preferred_eleme...  149 us
    another operation x54, other arithmetic  76.2 us
    dot_general x27, matrix products, second_pass(): lax.dot_general(probs_low, flat, (((0,), (0,)), ((), ())), preferred_elem...  54.9 us
    reshape x27, local copies, waits for them, and re-layouts, block_scores(): return (flat, scores.reshape(block_shifts, rows_here, ref_rows.shape[0]))  54 us
    dynamic_slice x54, local copies, waits for them, and re-layouts, block_scores(): lax.dynamic_slice_in_dim(sine, index * block_shifts, block_shifts)  47.8 us
    reduce_scatter x1, waiting for transfers between devices, on_device(): lax.psum_scatter(sums.reshape(classes_here, rotations, -1), 'dom', scatte...  20.1 us
    add x27, other arithmetic, second_pass(): weights_total = weights_total + jnp.sum(probs, axis=(0, 1))  18.5 us
    sub x54, local copies, waits for them, and re-layouts, second_pass(): probs = jnp.exp(scores - top[None, :, None]) / total[None, :, None]  18 us
  transfers between devices with their start and end apart: 8, of which 4 were waited for; matrix products, arithmetic and copies ran while one was open for 2% of the time, Pallas kernels for 0%

profile of v1, /device:TPU:0, one launch (start us, length us, event | category | flops | bytes accessed | tf_op | source)
XLA Modules:
  0.0 562.5 jit_solution(711071138619459089)
XLA Ops:
  7.7 4.1 collective-permute-start.4
  18.7 6.1 %collective-permute-done.1 = f32[8,36,256]{2,0,1:T(8,128)S(1)} collective-permute-done((f32[8,36,256]{2,0,1:T(8,128)S(1)}, f32[8,36,256]{2,0,1:T(8,128)S(1)}, u32[]{:S(2)}, u32[]{:S(2)}) %collective-permute-start.1) | collective-permute-done | bytes 294944 | tf_op jit(solution)/shard_map/ppermute | solution.py:60
  28.5 3.5 collective-permute-start.5
  32.9 10.8 %all_gather.3 = bf16[96,2048]{1,0:T(8,128)(2,1)S(1)} all-gather(bf16[96,512]{1,0:T(8,128)(2,1)} %param.7), channel_id=1, replica_groups=mesh['dom'=8,'cls'=4] {'cls'}, dimensions={1}, use_global_device_ids=true | all-gather | bytes 491520 | tf_op jit(solution)/shard_map/all_gather | solution.py:42
  52.9 3.9 gather_fusion
  65.0 131.2 %while.34 = (s32[]{:T(128)}, f32[96]{0:T(128)S(1)}, f32[96]{0:T(128)S(1)}, f32[96,1024]{1,0:T(8,128)}, f32[81,1024]{1,0:T(8,128)}, /*index=5*/f32[96,1024]{1,0:T...) while((s32[]{:T(128)}, f32[96]{0:T(128)S(1)}, ...), condition=%wide.wide.region_6.7_spmd.clone, body=%wide.wide.region_1.6_spmd.clone.sunk | while | flops 344789472 | bytes 5082850 | solution.py:106
  196.2 8.9 %pmax.7 = f32[96]{0:T(128)S(1)} all-reduce(f32[96]{0:T(128)S(1)} %get-tuple-element.342), channel_id=1, replica_groups=mesh['dom'=8,'cls'=4] {'cls'}, use_global_device_ids=true, to_apply=%region_7.8 | all-reduce | flops 96 | bytes 768 | tf_op jit(solution)/shard_map/pmax | solution.py:107
  205.1 8.3 %psum.14 = f32[96]{0:T(128)S(1)} all-reduce(f32[96]{0:T(128)S(1)} %exponential_multiply_fusion), channel_id=1, replica_groups=mesh['dom'=8,'cls'=4] {'cls'}, use_global_device_ids=true, to_apply=%region_8.9 | all-reduce | flops 96 | bytes 768 | tf_op jit(solution)/shard_map/psum | solution.py:108
  213.4 304.1 %while.35 = (s32[]{:T(128)}, f32[288,2048]{1,0:T(8,128)S(1)}, f32[288]{0:T(512)S(1)}, f32[96,1024]{1,0:T(8,128)}, f32[81,1024]{1,0:T(8,128)}, /*index=5*/f32[96,...) while((s32[]{:T(128)}, f32[288,2048]{1,0:T(8,128)S(1)}, ...), condition=%wide.wide.region_11.12_spmd.clone, body=%wide.wide.region_9.11_spmd.clone.sunk | while | flops 688315712 | bytes 11641178 | solution.py:127
  216.5 3.4 fusion.61
  227.7 3.4 fusion.61
  239.0 3.4 fusion.61
  261.5 3.4 fusion.61
  272.8 3.4 fusion.61
  284.1 3.4 fusion.61
  295.3 3.4 fusion.61
  306.6 3.4 fusion.61
  329.1 3.4 fusion.61
  351.6 3.4 fusion.61
  362.9 3.4 fusion.61
  374.2 3.4 fusion.61
  385.4 3.4 fusion.61
  396.7 3.4 fusion.61
  419.2 3.4 fusion.61
  441.7 3.4 fusion.61
  464.3 3.4 fusion.61
  475.5 3.4 fusion.61
  486.8 3.4 fusion.61
  498.0 3.4 fusion.61
  509.3 3.4 fusion.61
  519.2 14.6 %psum.15 = f32[8,36]{1,0:T(8,128)} all-reduce(f32[8,36]{1,0:T(8,128)S(1)} %reshape.211), channel_id=1, replica_groups=mesh['dom'=8,'cls'=4] {'dom'}, use_global_device_ids=true, to_apply=%region_13.14 | all-reduce | flops 288 | bytes 2304 | tf_op jit(solution)/shard_map/psum | solution.py:131
  533.8 20.1 %reduce-scatter.2.cloned.1.call-done = f32[8,36,256]{2,1,0:T(8,128)} async-done(((f32[8,36,2048]{2,1,0:T(8,128)}), f32[8,36,256]{2,1,0:T(8,128)}) %reduce-scatter.2.cloned.1.call-update) | async-done | bytes 294928 | tf_op jit(solution)/shard_map/reduce_scatter | solution.py:128
  (654 shorter events, 392.8 us)
Async XLA Ops:
  7.2 546.8 %reduce-scatter.2.cloned.1.call-start = ((), (), s32[]{:S(2)}) async-start(), calls=%async_computation.1 | async-start | bytes 2949120 | tf_op jit(solution)/shard_map/reduce_scatter | solution.py:128
  7.2 9.7 %collective-permute-start = (f32[8,36,256]{2,0,1:T(8,128)}, f32[8,36,256]{2,0,1:T(8,128)S(1)}, u32[]{:S(2)}, u32[]{:S(2)}) collective-permute-start(f32[8,36,256]{2,0,1:T(8,128)} %param.8), channel_id=1, source_target_pairs={{0,4},{4,8},{8,12},{12,16},{16,20},{20,24},{24,28},{28,0},{1,5},{5... | collective-permute-start | bytes 884744 | tf_op jit(solution)/shard_map/ppermute | solution.py:60
  7.7 20.7 %collective-permute-start.4 = (f32[8,36,256]{2,0,1:T(8,128)}, f32[8,36,256]{2,0,1:T(8,128)S(1)}, u32[]{:S(2)}, u32[]{:S(2)}) collective-permute-start(f32[8,36,256]{2,0,1:T(8,128)} %param.8), channel_id=1, source_target_pairs={{4,0},{8,4},{12,8},{16,12},{20,16},{24,20},{28,24},{0,28},{5,1},{9... | collective-permute-start | bytes 884744 | tf_op jit(solution)/shard_map/ppermute | solution.py:63
  16.9 7.9 %collective-permute-start.1 = (f32[8,36,256]{2,0,1:T(8,128)S(1)}, f32[8,36,256]{2,0,1:T(8,128)S(1)}, u32[]{:S(2)}, u32[]{:S(2)}) collective-permute-start(f32[8,36,256]{2,0,1:T(8,128)S(1)} %collective-permute-done), channel_id=1, source_target_pairs={{0,4},{4,8},{8,12},{12,16},{16,20},{20,24},{24,28},{28,0},{1,5},{5... | collective-permute-start | bytes 884744 | tf_op jit(solution)/shard_map/ppermute | solution.py:60
  24.8 8.1 %collective-permute-start.2 = (f32[8,36,256]{2,0,1:T(8,128)S(1)}, f32[8,36,256]{2,0,1:T(8,128)S(1)}, u32[]{:S(2)}, u32[]{:S(2)}) collective-permute-start(f32[8,36,256]{2,0,1:T(8,128)S(1)} %collective-permute-done.1), channel_id=1, source_target_pairs={{0,4},{4,8},{8,12},{12,16},{16,20},{20,24},{24,28},{28,0},{1,5},{5... | collective-permute-start | bytes 884744 | tf_op jit(solution)/shard_map/ppermute | solution.py:60
  25.4 24.6 %copy-start = (f32[8,36,256]{2,0,1:T(8,128)S(1)}, f32[8,36,256]{2,0,1:T(8,128)}, u32[]{:S(2)}) copy-start(f32[8,36,256]{2,0,1:T(8,128)} %param.8) | copy-start | bytes 884740
  28.5 16.2 %collective-permute-start.5 = (f32[8,36,256]{2,0,1:T(8,128)S(1)}, f32[8,36,256]{2,0,1:T(8,128)S(1)}, u32[]{:S(2)}, u32[]{:S(2)}) collective-permute-start(f32[8,36,256]{2,0,1:T(8,128)S(1)} %collective-permute-done.4), channel_id=1, source_target_pairs={{4,0},{8,4},{12,8},{16,12},{20,16},{24,20},{28,24},{0,28},{5,1},{9... | collective-permute-start | bytes 884744 | tf_op jit(solution)/shard_map/ppermute | solution.py:63
  32.9 14.2 %collective-permute-start.3 = (f32[8,36,256]{2,0,1:T(8,128)S(1)}, f32[8,36,256]{2,0,1:T(8,128)S(1)}, u32[]{:S(2)}, u32[]{:S(2)}) collective-permute-start(f32[8,36,256]{2,0,1:T(8,128)S(1)} %collective-permute-done.2), channel_id=1, source_target_pairs={{0,4},{4,8},{8,12},{12,16},{16,20},{20,24},{24,28},{28,0},{1,5},{5... | collective-permute-start | bytes 884744 | tf_op jit(solution)/shard_map/ppermute | solution.py:60
  44.7 7.5 %collective-permute-start.6 = (f32[8,36,256]{2,0,1:T(8,128)S(1)}, f32[8,36,256]{2,0,1:T(8,128)S(1)}, u32[]{:S(2)}, u32[]{:S(2)}) collective-permute-start(f32[8,36,256]{2,0,1:T(8,128)S(1)} %collective-permute-done.5), channel_id=1, source_target_pairs={{4,0},{8,4},{12,8},{16,12},{20,16},{24,20},{28,24},{0,28},{5,1},{9... | collective-permute-start | bytes 884744 | tf_op jit(solution)/shard_map/ppermute | solution.py:63
  52.9 3.9 copy-start.3
  58.9 3.8 copy-start.1
  62.7 1.0 copy-start.2
Sparse Core Ops, SparseCore 0:
  519.3 34.5 reduce-scatter.1
